TPU v7x, 32 devices: a whole 2x2x4 slice. The times are simulated.
32 devices in a mesh: ctx: 4 (over z), ep: 8 (over y, x, core).
Axes of the slice: x: 2, y: 2, z: 4, core: 2. Of those that a mesh axis runs over, the one named last changes fastest.
Arguments:
- out_grad: bfloat16 [64, 3584], P(('ctx', 'ep')), may hold values from -6 to 6
- expert_ids: int32 [64, 8], P(('ctx', 'ep')), may hold values from 0 to 31, all different within a row; in each aligned block of 16 rows (0 to 15, 16 to 31, ...) at most 7 rows name the same one
- gate_values: float32 [64, 8], P(('ctx', 'ep')), may hold values from 0.1 to 2.5
- hidden: bfloat16 [4, 32, 7, 1536], P(None, 'ep', None, 'ctx'), may hold values from -0.29882812 to 0.29882812
- w_down: bfloat16 [32, 1536, 3584], P('ep', 'ctx'), may hold values from -0.15625 to 0.15625
Outputs:
- hidden_grad: bfloat16 [4, 32, 7, 1536], P(None, 'ep', None, 'ctx')
- weight_grad: bfloat16 [32, 1536, 3584], P('ep', 'ctx')
- gate_grad: float32 [64, 8], P(('ctx', 'ep'))
Inputs may be any that keep to these rules, and one draw needn't show every extreme that they name: `expert_ids`: each token names 8 different experts. In each aligned block of 16 tokens no expert is named by more than 7 tokens.
All inputs are finite; a program needn't handle non-finite values.
Results may differ from a plain program's by a relative error of at most 0.012.
Values may be sent and summed in bfloat16 or wider, within the bound.
A program may use at most 64 MiB of HBM per device.

v0:
```python
import jax
import jax.numpy as jnp
from jax import lax
from jax.sharding import PartitionSpec as P


def route_places(group_ids, experts_all, capacity):
    flat_ids = group_ids.reshape(-1)
    onehot = (flat_ids[:, None] == jnp.arange(experts_all, dtype=jnp.int32)[None, :]).astype(
        jnp.int32
    )
    before = jnp.cumsum(onehot, axis=0) - onehot
    slot_index = jnp.sum(before * onehot, axis=1)
    return (flat_ids * capacity + slot_index).astype(jnp.int32)


def per_device(out_grad, expert_ids, gate_values, hidden, w_down):
    tok_dev, top_count = expert_ids.shape
    groups, exp_dev, capacity, width_part = hidden.shape
    model_width = out_grad.shape[1]
    ep_count = lax.axis_size("ep")
    ep_rank = lax.axis_index("ep")
    slots_dev = exp_dev * capacity
    experts_all = exp_dev * ep_count
    own_first = ep_rank * slots_dev
    slot_range = jnp.arange(slots_dev, dtype=jnp.int32)
    group_rows, group_ids, group_gates = (
        lax.all_gather(out_grad, "ep", axis=0, tiled=True),
        lax.all_gather(expert_ids, "ep", axis=0, tiled=True),
        lax.all_gather(gate_values.astype(jnp.bfloat16), "ep", axis=0, tiled=True).astype(
            gate_values.dtype
        ),
    )
    places = route_places(group_ids, experts_all, capacity)
    own_places = lax.dynamic_slice_in_dim(
        places, ep_rank * tok_dev * top_count, tok_dev * top_count
    )
    local_slot = places - own_first
    pick_mask = (local_slot[None, :] == slot_range[:, None]).astype(jnp.float32)
    slot_gates = jnp.sum(pick_mask * group_gates.reshape(1, -1), axis=1)
    by_token = pick_mask.reshape(slots_dev, -1, top_count).sum(axis=2).astype(jnp.bfloat16)
    slot_rows = jnp.dot(by_token, group_rows, preferred_element_type=jnp.float32).astype(
        jnp.bfloat16
    )
    stacked_rows = slot_rows.reshape(1, slots_dev, model_width)
    stacked_gates = slot_gates.reshape(1, slots_dev)
    whole_rows, whole_gates = (
        lax.all_gather(stacked_rows, "ctx", axis=0, tiled=True),
        lax.all_gather(stacked_gates.astype(jnp.bfloat16), "ctx", axis=0, tiled=True).astype(
            stacked_gates.dtype
        ),
    )
    row_count = whole_rows.shape[0]
    piece_view = whole_rows.reshape(row_count, exp_dev, capacity, model_width)
    gate_view = whole_gates.reshape(row_count, exp_dev, capacity)
    grad_in = jnp.einsum("necd,efd->necf", piece_view, w_down, preferred_element_type=jnp.float32)
    hid_piece = (gate_view[..., None] * grad_in).astype(jnp.bfloat16)
    gate_piece = jnp.sum(hidden.astype(jnp.float32) * grad_in, axis=3)
    scaled = (gate_view[..., None] * piece_view.astype(jnp.float32)).astype(jnp.bfloat16)
    grad_acc = jnp.einsum("necf,necd->efd", hidden, scaled, preferred_element_type=jnp.float32)
    hid_grad = hid_piece
    partial_value = gate_piece
    grad_acc, hid_grad, partial_value = (grad_acc, hid_grad, partial_value)
    whole_terms = lax.psum(partial_value, "ctx")
    own_terms = lax.dynamic_slice_in_dim(whole_terms, lax.axis_index("ctx"), 1, 0)
    score_table = lax.all_gather(own_terms.reshape(slots_dev), "ep", axis=0, tiled=True)
    lookup = (
        own_places[:, None] == jnp.arange(score_table.shape[0], dtype=jnp.int32)[None, :]
    ).astype(jnp.float32)
    gate_grad = jnp.sum(lookup * score_table[None, :], axis=1).reshape(tok_dev, top_count)
    return (hid_grad, grad_acc.astype(jnp.bfloat16), gate_grad)


def solution(mesh):
    placed = (
        P(("ctx", "ep"), None),
        P(("ctx", "ep"), None),
        P(("ctx", "ep"), None),
        P(None, "ep", None, "ctx"),
        P("ep", "ctx", None),
    )
    return jax.shard_map(
        per_device,
        mesh=mesh,
        in_specs=placed,
        out_specs=(P(None, "ep", None, "ctx"), P("ep", "ctx", None), P(("ctx", "ep"), None)),
        check_vma=False,
    )
```

profile of v0, /device:TPU:0, one launch (start us, length us, event | category | flops | bytes accessed | tf_op | source)
XLA Modules:
  0.0 119.2 jit_solution(10232744558941915128)
XLA Ops:
  0.6 0.0 copy-start
  0.7 1.3 %dynamic-slice.1 = u32[1]{0:T(128)} dynamic-slice(u32[32]{0:T(128)} %constant.42, u32[]{:T(128)S(6)} %add.22), dynamic_slice_sizes={1} | dynamic-slice | bytes 12
  2.6 1.2 %dynamic-slice = u32[1]{0:T(128)} dynamic-slice(u32[32]{0:T(128)} %constant.37, u32[]{:T(128)S(6)} %add.22), dynamic_slice_sizes={1} | dynamic-slice | bytes 12
  4.5 0.7 convert_bitcast_fusion
  5.2 10.3 %all-gather.3 = bf16[8,2,8]{2,1,0:T(2,128)(2,1)S(1)} all-gather(bf16[1,2,8]{2,1,0:T(2,128)(2,1)S(1)} %convert_bitcast_fusion), channel_id=1, replica_groups=mesh['ctx'=4,'ep'=8] {'ep'}, dimensions={0}, use_global_device_ids=true | all-gather | bytes 288 | tf_op jit(solution)/shard_map/all_gather | solution.py:30
  15.4 0.1 reshape.61
  15.5 8.9 %all-gather.2 = s32[8,2,8]{2,1,0:T(2,128)S(1)} all-gather(s32[1,2,8]{2,1,0:T(2,128)} %bitcast.35), channel_id=1, replica_groups=mesh['ctx'=4,'ep'=8] {'ep'}, dimensions={0}, use_global_device_ids=true | all-gather | bytes 576 | tf_op jit(solution)/shard_map/all_gather | solution.py:29
  24.4 0.1 reshape.56
  24.5 0.1 fusion.9
  24.6 0.2 reduce_window_sum.11
  24.8 0.2 select_reduce_fusion
  25.0 0.1 select_reduce_fusion.2
  25.1 0.2 dynamic-update-slice
  25.4 11.9 %all-reduce = bf16[112]{0:T(256)(128)(2,1)S(1)} all-reduce(bf16[112]{0:T(256)(128)(2,1)S(1)} %dynamic-update-slice), channel_id=2, replica_groups=mesh['ctx'=4,'ep'=8] {'ctx'}, use_global_device_ids=true, to_apply=%add | all-reduce | flops 112 | bytes 448
  37.3 0.1 dynamic_slice.6
  37.4 0.1 reshape.62
  37.5 0.1 reduce_sum.49
  37.6 0.1 convert_reduce_fusion
  37.7 0.1 copy.33
  37.8 8.4 %all-gather.4 = bf16[8,2,3584]{2,1,0:T(2,128)(2,1)S(1)} all-gather(bf16[1,2,3584]{2,1,0:T(2,128)(2,1)} %bitcast.34), channel_id=1, replica_groups=mesh['ctx'=4,'ep'=8] {'ep'}, dimensions={0}, use_global_device_ids=true | all-gather | bytes 129024 | tf_op jit(solution)/shard_map/all_gather | solution.py:28
  46.3 0.2 fusion.3
  46.5 19.8 %all-gather.5 = bf16[4,28,3584]{2,1,0:T(8,128)(2,1)S(1)} all-gather(bf16[1,28,3584]{2,1,0:T(8,128)(2,1)S(1)} %fusion.3), channel_id=3, replica_groups=mesh['ctx'=4,'ep'=8] {'ctx'}, dimensions={0}, use_global_device_ids=true | all-gather | bytes 1003520 | tf_op jit(solution)/shard_map/all_gather | solution.py:48
  66.3 0.6 copy.34
  67.0 7.6 %multiply_reduce_fusion = (f32[4,4,7]{0,2,1:T(8,128)S(1)}, bf16[4,4,7,384]{3,0,2,1:T(4,128)(2,1)S(1)}) fusion(bf16[4,4,7,384]{3,1,2,0:T(4,128)(2,1)} %param.8, f32[4,4,7]{0,2,1:T(8,128)S(1)} %copy.33, bf16[4,4,7,3584]{3,0,2,1:T(4,128)(2,1)S(1)} %bitcast.31, bf16[4,384,3584]{2,1,0:T(8,128)(2,1)} %param.9), kind=kOutput, calls=%fused_computation.9 | convolution fusion | flops 308496256 | bytes 11985792 | tf_op jit(solution)/shard_map/necd,efd->necf/dot_general | solution.py:56
  74.6 0.1 copy.43
  74.7 10.0 %psum.7 = f32[4,4,7]{2,0,1:T(4,128)S(1)} all-reduce(f32[4,4,7]{2,0,1:T(4,128)S(1)} %copy.43), channel_id=1, replica_groups=mesh['ctx'=4,'ep'=8] {'ctx'}, use_global_device_ids=true, to_apply=%region_5.6 | all-reduce | flops 112 | bytes 896 | tf_op jit(solution)/shard_map/psum | solution.py:64
  84.7 0.1 reshape.71
  84.7 0.2 dynamic-update-slice.1
  84.9 11.8 %all-reduce.1 = f32[224]{0:T(256)S(1)} all-reduce(f32[224]{0:T(256)S(1)} %dynamic-update-slice.1), channel_id=1, replica_groups=mesh['ctx'=4,'ep'=8] {'ep'}, use_global_device_ids=true, to_apply=%add.1 | all-reduce | flops 224 | bytes 1792
  96.7 0.2 select_reduce_fusion.1
  96.9 0.6 reshape.60
  97.5 0.7 copy.39
  98.2 0.0 copy-done
  98.2 6.3 %fusion = bf16[4,384,3584]{1,2,0:T(8,128)(2,1)} fusion(bf16[4,4,7,3584]{3,0,2,1:T(4,128)(2,1)S(1)} %bitcast.32, f32[4,4,7]{0,2,1:T(8,128)S(1)} %copy.33, bf16[4,4,7,384]{3,1,2,0:T(4,128)(2,1)S(1)} %copy-done), kind=kOutput, calls=%fused_computation.1 | convolution fusion | flops 314990592 | bytes 11899328 | tf_op jit(solution)/shard_map/necf,necd->efd/dot_general | solution.py:60
  104.6 14.6 %copy.40 = bf16[4,384,3584]{2,1,0:T(8,128)(2,1)} copy(bf16[4,384,3584]{1,2,0:T(8,128)(2,1)} %fusion) | data formatting | bytes 22020096
  (7 shorter events, 0.1 us)
Async XLA Ops:
  0.6 97.6 %copy-start = (bf16[4,4,7,384]{3,1,2,0:T(4,128)(2,1)S(1)}, bf16[4,4,7,384]{3,1,2,0:T(4,128)(2,1)}, u32[]{:S(2)}) copy-start(bf16[4,4,7,384]{3,1,2,0:T(4,128)(2,1)} %param.8) | copy-start | bytes 258052
where the time goes:
time: 120 us; the launch traced here: 119 us
  blocking collectives  81.1 us (68%)
  local copies, waits for them, and re-layouts  20.3 us (17%)
  matrix products  14.2 us (12%)
  between operations  2.04 us (2%)
  other arithmetic  1.55 us (1%)
    unnamed x2, blocking collectives  23.7 us
    all_gather x1, blocking collectives, per_device(): lax.all_gather(stacked_rows, 'ctx', axis=0, tiled=True)  19.8 us
    unnamed x12, local copies, waits for them, and re-layouts  18.4 us
    all_gather x1, blocking collectives, per_device(): lax.all_gather(gate_values.astype(jnp.bfloat16), 'ep', axis=0, tiled=True)  10.3 us
    psum x1, blocking collectives, per_device(): whole_terms = lax.psum(partial_value, 'ctx')  9.95 us
    all_gather x1, blocking collectives, per_device(): lax.all_gather(expert_ids, 'ep', axis=0, tiled=True)  8.91 us
    all_gather x1, blocking collectives, per_device(): lax.all_gather(out_grad, 'ep', axis=0, tiled=True)  8.44 us
    dot_general x1, matrix products, per_device(): jnp.einsum('necd,efd->necf', piece_view, w_down, preferred_element_type=j...  7.58 us

commit v1 on v0

--- a/solution.py
+++ b/solution.py
@@ -1,7 +1,224 @@
+import functools
 import jax
 import jax.numpy as jnp
 from jax import lax
+from jax.experimental import pallas as pl
+from jax.experimental.pallas import tpu as pltpu
 from jax.sharding import PartitionSpec as P
+
+LANES = 128
+VMEM_BUDGET = 40 << 20
+MESH = pl.DeviceIdType.MESH
+HIGHEST = lax.Precision.HIGHEST
+
+
+def exchange_kernel(
+    sizes, pack_ref, hid_ref, w_ref,
+    hid_grad_ref, by_token_ref, rows_ref, gates_ref, route_ref,
+    rows_in, w_in, part, parts_in,
+    w_sem, own_sem, send_sem, recv_sem, send2_sem, recv2_sem,
+):
+    ctx_count, ep_count, tok_dev, top, groups, exp_dev, capacity, width = sizes
+    count = ctx_count * ep_count
+    tokens = count * tok_dev
+    group_tok = tokens // groups
+    features = rows_ref.shape[1]
+    ctx, ep = lax.axis_index("ctx"), lax.axis_index("ep")
+    me = ctx * ep_count + ep
+    weights = [
+        pltpu.make_async_copy(w_ref.at[e], w_in.at[e], w_sem.at[e]) for e in range(exp_dev)
+    ]
+    for copy in weights:
+        copy.start()
+    own = pltpu.make_async_copy(pack_ref, rows_in.at[me], own_sem)
+    own.start()
+
+    peers = []
+    for step in range(1, count):
+        peer = lax.rem(me + step, count)
+        peers.append((peer // ep_count, lax.rem(peer, ep_count)))
+    barrier = pltpu.get_barrier_semaphore()
+    for peer in peers:
+        pl.semaphore_signal(barrier, inc=1, device_id=peer, device_id_type=MESH)
+    pl.semaphore_wait(barrier, count - 1)
+    sends = [
+        pltpu.make_async_remote_copy(
+            src_ref=pack_ref, dst_ref=rows_in.at[me], send_sem=send_sem.at[i],
+            recv_sem=recv_sem.at[i], device_id=peer, device_id_type=MESH,
+        )
+        for i, peer in enumerate(peers)
+    ]
+    for copy in sends:
+        copy.start()
+
+    pad = 8
+    hid = []
+    for e in range(exp_dev):
+        pieces = []
+        for g in range(groups):
+            piece = hid_ref[g, e].astype(jnp.float32)
+            pieces.append(
+                jnp.concatenate([piece, jnp.zeros((pad - capacity, width), jnp.float32)], axis=0)
+            )
+        hid.append(jnp.concatenate(pieces, axis=0))
+
+    own.wait()
+    for copy in sends:
+        copy.wait_recv()
+
+    gathered = rows_in[...].reshape(tokens, features + LANES)
+    rows_ref[...] = gathered[:, :features]
+    meta = gathered[:, features:].astype(jnp.float32)
+    meta_t = meta.T
+    ids_t = meta_t[:top].astype(jnp.int32)
+    gates_t = meta_t[top:2 * top]
+    tok_a = lax.broadcasted_iota(jnp.int32, (tokens, tokens), 0)
+    tok_b = lax.broadcasted_iota(jnp.int32, (tokens, tokens), 1)
+    earlier = ((tok_a < tok_b) & (tok_a // group_tok == tok_b // group_tok)).astype(jnp.float32)
+    row_slot = lax.broadcasted_iota(jnp.int32, (groups * pad, tokens), 0)
+    row_group = lax.broadcasted_iota(jnp.int32, (groups * pad, tokens), 1) // group_tok
+
+    members, gate_rows = [], []
+    for e in range(exp_dev):
+        named = ids_t == ep * exp_dev + e
+        members.append(jnp.sum(jnp.where(named, 1.0, 0.0), axis=0, keepdims=True))
+        gate_rows.append(jnp.sum(jnp.where(named, gates_t, 0.0), axis=0, keepdims=True))
+    member = jnp.concatenate(members + [jnp.zeros((8 - exp_dev, tokens), jnp.float32)], axis=0)
+    gate = jnp.concatenate(gate_rows + [jnp.zeros((8 - exp_dev, tokens), jnp.float32)], axis=0)
+    slots = jnp.dot(member, earlier, preferred_element_type=jnp.float32).astype(jnp.int32)
+    gates_ref[...] = jnp.concatenate(
+        [gate, jnp.zeros((LANES - 8, tokens), jnp.float32)], axis=0
+    ).T
+
+    rows = rows_ref[...]
+    for e in range(exp_dev):
+        place = jnp.where(member[e:e + 1] > 0, row_group[:1] * pad + slots[e:e + 1], -1)
+        pick = jnp.where(row_slot == place, 1.0, 0.0)
+        by_token = lax.dot_general(
+            hid[e].astype(jnp.bfloat16), pick.astype(jnp.bfloat16), (((0,), (0,)), ((), ())),
+            preferred_element_type=jnp.float32,
+        )
+        by_token_ref[e] = by_token.astype(jnp.bfloat16)
+        weights[e].wait()
+        grad = lax.dot_general(
+            w_in[e], rows, (((1,), (1,)), ((), ())), preferred_element_type=jnp.float32
+        )
+        part[e:e + 1, :] = jnp.sum(by_token * grad, axis=0, keepdims=True)
+        gated = grad * gate[e:e + 1]
+        slot_grad = lax.dot_general(
+            pick.astype(jnp.bfloat16), gated.astype(jnp.bfloat16), (((1,), (1,)), ((), ())),
+            preferred_element_type=jnp.float32,
+        )
+        for g in range(groups):
+            hid_grad_ref[g, e] = slot_grad[g * pad:g * pad + capacity].astype(jnp.bfloat16)
+
+    returns = [
+        pltpu.make_async_remote_copy(
+            src_ref=part, dst_ref=parts_in.at[me], send_sem=send2_sem.at[i],
+            recv_sem=recv2_sem.at[i], device_id=peer, device_id_type=MESH,
+        )
+        for i, peer in enumerate(peers)
+    ]
+    for copy in returns:
+        copy.start()
+    for copy in sends:
+        copy.wait_send()
+    for copy in returns:
+        copy.wait_recv()
+    mine = part[...]
+    result = jnp.zeros((top, tokens), jnp.float32)
+    for p in range(ep_count):
+        total = jnp.zeros(mine.shape, jnp.float32)
+        for c in range(ctx_count):
+            d = c * ep_count + p
+            total = total + jnp.where(d == me, mine, parts_in[d])
+        for e in range(exp_dev):
+            result = result + jnp.where(ids_t == p * exp_dev + e, total[e:e + 1], 0.0)
+    route_ref[...] = result
+    for copy in returns:
+        copy.wait_send()
+
+
+def weight_kernel(exp_dev, chunk, by_token_ref, rows_ref, gates_ref, out_ref):
+    lane = lax.broadcasted_iota(jnp.int32, gates_ref.shape, 1)
+    gate = jnp.sum(
+        jnp.where(lane == pl.program_id(0), gates_ref[...], 0.0), axis=1, keepdims=True
+    )
+    left = by_token_ref[0]
+    for at in range(0, out_ref.shape[2], chunk):
+        scaled = (gate * rows_ref[:, at:at + chunk].astype(jnp.float32)).astype(jnp.bfloat16)
+        out_ref[0, :, at:at + chunk] = jnp.dot(
+            left, scaled, preferred_element_type=jnp.float32
+        ).astype(jnp.bfloat16)
+
+
+def fused_device(out_grad, expert_ids, gate_values, hidden, w_down):
+    tok_dev, top = expert_ids.shape
+    groups, exp_dev, capacity, width = hidden.shape
+    features = out_grad.shape[1]
+    ctx_count, ep_count = lax.axis_size("ctx"), lax.axis_size("ep")
+    count = ctx_count * ep_count
+    tokens = count * tok_dev
+    pack = jnp.concatenate(
+        [
+            out_grad,
+            expert_ids.astype(jnp.bfloat16),
+            gate_values.astype(jnp.bfloat16),
+            jnp.zeros((tok_dev, LANES - 2 * top), jnp.bfloat16),
+        ],
+        axis=1,
+    )
+    sizes = (ctx_count, ep_count, tok_dev, top, groups, exp_dev, capacity, width)
+    vmem = pl.BlockSpec(memory_space=pltpu.VMEM)
+    hid_grad, by_token, rows, gates, routes = pl.pallas_call(
+        functools.partial(exchange_kernel, sizes),
+        out_shape=(
+            jax.ShapeDtypeStruct(hidden.shape, jnp.bfloat16),
+            jax.ShapeDtypeStruct((exp_dev, width, tokens), jnp.bfloat16),
+            jax.ShapeDtypeStruct((tokens, features), jnp.bfloat16),
+            jax.ShapeDtypeStruct((tokens, LANES), jnp.float32),
+            jax.ShapeDtypeStruct((top, tokens), jnp.float32),
+        ),
+        in_specs=[vmem, vmem, pl.BlockSpec(memory_space=pl.ANY)],
+        out_specs=(vmem,) * 5,
+        scratch_shapes=[
+            pltpu.VMEM((count, tok_dev, features + LANES), jnp.bfloat16),
+            pltpu.VMEM(w_down.shape, jnp.bfloat16),
+            pltpu.VMEM((exp_dev, tokens), jnp.float32),
+            pltpu.VMEM((count, exp_dev, tokens), jnp.float32),
+            pltpu.SemaphoreType.DMA((exp_dev,)),
+            pltpu.SemaphoreType.DMA,
+            pltpu.SemaphoreType.DMA((count - 1,)),
+            pltpu.SemaphoreType.DMA((count - 1,)),
+            pltpu.SemaphoreType.DMA((count - 1,)),
+            pltpu.SemaphoreType.DMA((count - 1,)),
+        ],
+        compiler_params=pltpu.CompilerParams(
+            collective_id=0, has_side_effects=True, vmem_limit_bytes=56 << 20
+        ),
+        name="exchange",
+    )(pack, hidden, w_down)
+    chunk = features
+    for pieces in range(1, features // LANES + 1):
+        if features % (pieces * LANES) == 0 and features // pieces <= 4 * LANES:
+            chunk = features // pieces
+            break
+    weight_grad = pl.pallas_call(
+        functools.partial(weight_kernel, exp_dev, chunk),
+        grid=(exp_dev,),
+        out_shape=jax.ShapeDtypeStruct(w_down.shape, jnp.bfloat16),
+        in_specs=[
+            pl.BlockSpec((1, width, tokens), lambda e: (e, 0, 0)),
+            pl.BlockSpec((tokens, features), lambda e: (0, 0)),
+            pl.BlockSpec((tokens, LANES), lambda e: (0, 0)),
+        ],
+        out_specs=pl.BlockSpec((1, width, features), lambda e: (e, 0, 0)),
+        compiler_params=pltpu.CompilerParams(vmem_limit_bytes=56 << 20),
+        name="weight",
+    )(by_token, rows, gates)
+    me = lax.axis_index("ctx") * ep_count + lax.axis_index("ep")
+    gate_grad = lax.dynamic_slice_in_dim(routes, me * tok_dev, tok_dev, 1).T
+    return hid_grad, weight_grad, gate_grad
 
 
 def route_places(group_ids, experts_all, capacity):
@@ -14,7 +231,7 @@
     return (flat_ids * capacity + slot_index).astype(jnp.int32)
 
 
-def per_device(out_grad, expert_ids, gate_values, hidden, w_down):
+def plain_device(out_grad, expert_ids, gate_values, hidden, w_down):
     tok_dev, top_count = expert_ids.shape
     groups, exp_dev, capacity, width_part = hidden.shape
     model_width = out_grad.shape[1]
@@ -71,6 +288,16 @@
     return (hid_grad, grad_acc.astype(jnp.bfloat16), gate_grad)
 
 
+def per_device(out_grad, expert_ids, gate_values, hidden, w_down):
+    count = lax.axis_size("ctx") * lax.axis_size("ep")
+    tokens = count * out_grad.shape[0]
+    exp_dev = hidden.shape[1]
+    held = 3 * 2 * tokens * out_grad.shape[1] + 2 * w_down.size + 32 * count * tokens
+    whole_tiles = out_grad.shape[1] % LANES == 0 and exp_dev <= 8 and hidden.shape[2] <= 8
+    body = fused_device if held <= VMEM_BUDGET and whole_tiles else plain_device
+    return body(out_grad, expert_ids, gate_values, hidden, w_down)
+
+
 def solution(mesh):
     placed = (
         P(("ctx", "ep"), None),

time: 120 us -> 50 us (0.42)
  blocking collectives: 81.1 us -> 0 us
  Pallas kernels: 0 us -> 41.7 us
  local copies, waits for them, and re-layouts: 20.3 us -> 5.89 us
  matrix products: 14.2 us -> 0 us
  between operations: 2.04 us -> 0.65 us
    all_gather x4 -> x0, blocking collectives: 47.4 us -> none  [the longest x1 19.8 us: per_device(): lax.all_gather(stacked_rows, 'ctx', axis=0, tiled=True)]
    pallas_call x0 -> x2, Pallas kernels: none -> 41.7 us  [the longest x1 34.7 us: fused_device(): pl.pallas_call(functools.partial(exchange_kernel, sizes), out_shape=(jax....]
    unnamed x2 -> x0, blocking collectives: 23.7 us -> none
    unnamed x12 -> x3, local copies, waits for them, and re-layouts: 18.4 us -> 3.74 us
    dot_general x3 -> x0, matrix products: 14.2 us -> none  [the longest x1 7.58 us: per_device(): jnp.einsum('necd,efd->necf', piece_view, w_down, preferred_element_type=j...]
    psum x1 -> x0, blocking collectives: 9.95 us -> none  [per_device(): whole_terms = lax.psum(partial_value, 'ctx')]
    concatenate x0 -> x1, local copies, waits for them, and re-layouts: none -> 1.4 us  [fused_device(): jnp.concatenate([out_grad, expert_ids.astype(jnp.bfloat16), gate_values.a...]
    convert_element_type x1 -> x2, other arithmetic: 0.08 us -> 1.36 us  [the longest x1 0.68 us: fused_device(): expert_ids.astype(jnp.bfloat16)]
where the time goes in v1:
time: 50 us; the launch traced here: 49.6 us
  Pallas kernels  41.7 us (83%)
  local copies, waits for them, and re-layouts  5.89 us (12%)
  other arithmetic  1.36 us (3%)
  between operations  0.65 us (1%)
    pallas_call x1, Pallas kernels, fused_device(): pl.pallas_call(functools.partial(exchange_kernel, sizes), out_shape=(jax....  34.7 us
    pallas_call x1, Pallas kernels, fused_device(): pl.pallas_call(functools.partial(weight_kernel, exp_dev, chunk), grid=(ex...  7.02 us
    unnamed x3, local copies, waits for them, and re-layouts  3.74 us
    concatenate x1, local copies, waits for them, and re-layouts, fused_device(): jnp.concatenate([out_grad, expert_ids.astype(jnp.bfloat16), gate_values.a...  1.4 us

profile of v1, /device:TPU:0, one launch (start us, length us, event | category | flops | bytes accessed | tf_op | source)
XLA Modules:
  0.0 49.6 jit_solution(17176471851955795429)
XLA Ops:
  0.6 0.7 %convert_element_type.6 = bf16[2,8]{1,0:T(2,128)(2,1)S(1)} convert(s32[2,8]{1,0:T(2,128)} %param.6) | non-fusion elementwise | flops 16 | bytes 96 | tf_op jit(solution)/shard_map/convert_element_type | solution.py:165
  1.3 0.7 %convert_element_type.7 = bf16[2,8]{1,0:T(2,128)(2,1)S(1)} convert(f32[2,8]{1,0:T(2,128)} %param.7) | non-fusion elementwise | flops 16 | bytes 96 | tf_op jit(solution)/shard_map/convert_element_type | solution.py:166
  2.0 1.4 %concatenate.3.pack_ref = bf16[2,3712]{1,0:T(2,128)(2,1)} concatenate(bf16[2,3584]{1,0:T(2,128)(2,1)} %param.5, bf16[2,8]{1,0:T(2,128)(2,1)S(1)} %convert_element_type.6, bf16[2,8]{1,0:T(2,128)(2,1)S(1)} %convert_element_type.7, bf16[2,112]{1,0:T(2,128)(2,1)S(1)} %broadcast_in_dim.3), dimensions={1} | concatenate | bytes 29696 | tf_op jit(solution)/shard_map/concatenate | solution.py:162
  3.4 1.5 %copy.8.hid_ref = bf16[4,4,7,384]{3,2,1,0:T(8,128)(2,1)} copy(bf16[4,4,7,384]{3,1,2,0:T(4,128)(2,1)} %param.8) | data formatting | bytes 172032 | tf_op args[3]
  4.9 34.7 %exchange.1 = (bf16[4,4,7,384]{3,2,1,0:T(8,128)(2,1)}, bf16[4,384,64]{2,1,0:T(8,128)(2,1)}, bf16[64,3584]{1,0:T(8,128)(2,1)}, f32[64,128]{1,0:T(8,128)}, f32[8,64]{1,0:T(8,128)}) custom-call(bf16[2,3712]{1,0:T(2,128)(2,1)} %concatenate.3.pack_ref, bf16[4,4,7,384]{3,2,1,0:T(8,128)(2,1)} %copy.8.hid_ref, bf16[4,384,3584]{2,1,0:T(8,128)(2,1)} %w_ref.1), custom_call_target="tpu_custom_call" | custom-call | tf_op jit(solution)/shard_map/exchange/pallas_call | solution.py:173
  39.6 1.6 %copy.9 = bf16[4,4,7,384]{3,1,2,0:T(4,128)(2,1)} copy(bf16[4,4,7,384]{3,2,1,0:T(8,128)(2,1)} %get-tuple-element.13) | data formatting | bytes 172032
  41.2 0.7 %dynamic-slice_bitcast_fusion = f32[2,8]{0,1:T(8,128)S(1)} fusion(f32[8,64]{1,0:T(8,128)} %get-tuple-element.12, s32[]{:T(128)S(6)} %select_n.3), kind=kLoop, calls=%fused_computation | loop fusion | bytes 132 | tf_op jit(solution)/shard_map/transpose | solution.py:220
  42.0 0.6 %copy.10 = f32[2,8]{1,0:T(2,128)} copy(f32[2,8]{0,1:T(8,128)S(1)} %dynamic-slice_bitcast_fusion) | data formatting | bytes 128
  42.6 7.0 %weight.1 = bf16[4,384,3584]{2,1,0:T(8,128)(2,1)} custom-call(bf16[4,384,64]{2,1,0:T(8,128)(2,1)} %get-tuple-element.9.by_token_ref, bf16[64,3584]{1,0:T(8,128)(2,1)} %get-tuple-element.10.rows_ref, f32[64,128]{1,0:T(8,128)} %get-tuple-element.11.gates_ref), custom_call_target="tpu_custom_call" | custom-call | tf_op jit(solution)/shard_map/weight/pallas_call | solution.py:206
  (1 shorter events, 0.0 us)

commit v2 on v1

--- a/solution.py
+++ b/solution.py
@@ -13,10 +13,10 @@
 
 
 def exchange_kernel(
-    sizes, pack_ref, hid_ref, w_ref,
+    sizes, grad_ref, ids_ref, gate_ref, hid_ref, w_ref,
     hid_grad_ref, by_token_ref, rows_ref, gates_ref, route_ref,
-    rows_in, w_in, part, parts_in,
-    w_sem, own_sem, send_sem, recv_sem, send2_sem, recv2_sem,
+    pack, rows_in, w_in, part, parts_in,
+    w_sem, own_sem, send_sem, recv_sem, pass_sem, passed_sem, send2_sem, recv2_sem,
 ):
     ctx_count, ep_count, tok_dev, top, groups, exp_dev, capacity, width = sizes
     count = ctx_count * ep_count
@@ -25,92 +25,107 @@
     features = rows_ref.shape[1]
     ctx, ep = lax.axis_index("ctx"), lax.axis_index("ep")
     me = ctx * ep_count + ep
+
+    def place_of(d):
+        return (d // ep_count, lax.rem(d, ep_count))
+
+    def rows_of(d):
+        return rows_in.at[d]
+
+    peers = [place_of(lax.rem(me + step, count)) for step in range(1, count)]
+    barrier = pltpu.get_barrier_semaphore()
+    for peer in peers:
+        pl.semaphore_signal(barrier, inc=1, device_id=peer, device_id_type=MESH)
     weights = [
         pltpu.make_async_copy(w_ref.at[e], w_in.at[e], w_sem.at[e]) for e in range(exp_dev)
     ]
     for copy in weights:
         copy.start()
-    own = pltpu.make_async_copy(pack_ref, rows_in.at[me], own_sem)
+    pack[...] = jnp.concatenate(
+        [
+            grad_ref[...],
+            ids_ref[...].astype(jnp.float32).astype(jnp.bfloat16),
+            gate_ref[...].astype(jnp.bfloat16),
+            jnp.zeros((tok_dev, LANES - 2 * top), jnp.bfloat16),
+        ],
+        axis=1,
+    )
+    pl.semaphore_wait(barrier, count - 1)
+
+    partner = place_of(me + 1 - 2 * lax.rem(me, 2))
+
+    def send(src, d, peer, one, two):
+        return pltpu.make_async_remote_copy(
+            src_ref=src, dst_ref=rows_of(d), send_sem=one, recv_sem=two,
+            device_id=peer, device_id_type=MESH,
+        )
+
+    half = count // 2
+    sends = [
+        send(pack, me, place_of(lax.rem(me + 2 * i, count)), send_sem.at[i - 1], recv_sem.at[i - 1])
+        for i in range(1, half)
+    ]
+    swaps = [send(pack, me, partner, pass_sem.at[0], passed_sem.at[0])]
+    for copy in sends + swaps:
+        copy.start()
+    own = pltpu.make_async_copy(pack, rows_of(me), own_sem)
     own.start()
 
-    peers = []
-    for step in range(1, count):
-        peer = lax.rem(me + step, count)
-        peers.append((peer // ep_count, lax.rem(peer, ep_count)))
-    barrier = pltpu.get_barrier_semaphore()
-    for peer in peers:
-        pl.semaphore_signal(barrier, inc=1, device_id=peer, device_id_type=MESH)
-    pl.semaphore_wait(barrier, count - 1)
-    sends = [
-        pltpu.make_async_remote_copy(
-            src_ref=pack_ref, dst_ref=rows_in.at[me], send_sem=send_sem.at[i],
-            recv_sem=recv_sem.at[i], device_id=peer, device_id_type=MESH,
-        )
-        for i, peer in enumerate(peers)
-    ]
-    for copy in sends:
-        copy.start()
-
     pad = 8
-    hid = []
-    for e in range(exp_dev):
-        pieces = []
-        for g in range(groups):
-            piece = hid_ref[g, e].astype(jnp.float32)
-            pieces.append(
-                jnp.concatenate([piece, jnp.zeros((pad - capacity, width), jnp.float32)], axis=0)
-            )
-        hid.append(jnp.concatenate(pieces, axis=0))
-
-    own.wait()
-    for copy in sends:
-        copy.wait_recv()
-
-    gathered = rows_in[...].reshape(tokens, features + LANES)
-    rows_ref[...] = gathered[:, :features]
-    meta = gathered[:, features:].astype(jnp.float32)
-    meta_t = meta.T
-    ids_t = meta_t[:top].astype(jnp.int32)
-    gates_t = meta_t[top:2 * top]
+    filler = jnp.zeros((pad - exp_dev, width), jnp.float32)
+    pieces = []
+    for g in range(groups):
+        for s in range(capacity):
+            pieces += [hid_ref[g, s].astype(jnp.float32)] + ([filler] if pad > exp_dev else [])
+    hid = jnp.concatenate(pieces, axis=0).astype(jnp.bfloat16)
+    slot_rows = groups * capacity * pad
     tok_a = lax.broadcasted_iota(jnp.int32, (tokens, tokens), 0)
     tok_b = lax.broadcasted_iota(jnp.int32, (tokens, tokens), 1)
     earlier = ((tok_a < tok_b) & (tok_a // group_tok == tok_b // group_tok)).astype(jnp.float32)
-    row_slot = lax.broadcasted_iota(jnp.int32, (groups * pad, tokens), 0)
-    row_group = lax.broadcasted_iota(jnp.int32, (groups * pad, tokens), 1) // group_tok
-
+    row_slot = lax.broadcasted_iota(jnp.int32, (slot_rows, tokens), 0)
+    first = lax.broadcasted_iota(jnp.int32, (1, tokens), 1) // group_tok * (capacity * pad)
+
+    for i in range(1, half):
+        sends[i - 1].wait_recv()
+        source = lax.rem(me - 2 * i + count, count)
+        copy = send(rows_of(source), source, partner, pass_sem.at[i], passed_sem.at[i])
+        copy.start()
+        swaps.append(copy)
+    own.wait()
+    for copy in swaps:
+        copy.wait_recv()
+
+    gathered = rows_in[...].reshape(tokens, features + LANES)
+    rows_ref[...] = gathered[:, :features]
+    meta_t = gathered[:, features:].astype(jnp.float32).T
+    ids_t = meta_t[:top].astype(jnp.int32)
+    gates_t = meta_t[top:2 * top]
     members, gate_rows = [], []
     for e in range(exp_dev):
         named = ids_t == ep * exp_dev + e
         members.append(jnp.sum(jnp.where(named, 1.0, 0.0), axis=0, keepdims=True))
         gate_rows.append(jnp.sum(jnp.where(named, gates_t, 0.0), axis=0, keepdims=True))
-    member = jnp.concatenate(members + [jnp.zeros((8 - exp_dev, tokens), jnp.float32)], axis=0)
-    gate = jnp.concatenate(gate_rows + [jnp.zeros((8 - exp_dev, tokens), jnp.float32)], axis=0)
+    empty = [jnp.zeros((1, tokens), jnp.float32)] * (pad - exp_dev)
+    member = jnp.concatenate(members + empty, axis=0)
+    gate = jnp.concatenate(gate_rows + empty, axis=0)
     slots = jnp.dot(member, earlier, preferred_element_type=jnp.float32).astype(jnp.int32)
-    gates_ref[...] = jnp.concatenate(
-        [gate, jnp.zeros((LANES - 8, tokens), jnp.float32)], axis=0
-    ).T
-
-    rows = rows_ref[...]
+    picks = []
     for e in range(exp_dev):
-        place = jnp.where(member[e:e + 1] > 0, row_group[:1] * pad + slots[e:e + 1], -1)
-        pick = jnp.where(row_slot == place, 1.0, 0.0)
+        place = jnp.where(member[e:e + 1] > 0, first + slots[e:e + 1] * pad + e, -1)
+        picks.append(jnp.where(row_slot == place, 1.0, 0.0).astype(jnp.bfloat16))
+
+    gated = []
+    for e in range(exp_dev):
         by_token = lax.dot_general(
-            hid[e].astype(jnp.bfloat16), pick.astype(jnp.bfloat16), (((0,), (0,)), ((), ())),
-            preferred_element_type=jnp.float32,
+            hid, picks[e], (((0,), (0,)), ((), ())), preferred_element_type=jnp.float32
         )
         by_token_ref[e] = by_token.astype(jnp.bfloat16)
         weights[e].wait()
         grad = lax.dot_general(
-            w_in[e], rows, (((1,), (1,)), ((), ())), preferred_element_type=jnp.float32
+            w_in[e], rows_ref[...], (((1,), (1,)), ((), ())), preferred_element_type=jnp.float32
         )
         part[e:e + 1, :] = jnp.sum(by_token * grad, axis=0, keepdims=True)
-        gated = grad * gate[e:e + 1]
-        slot_grad = lax.dot_general(
-            pick.astype(jnp.bfloat16), gated.astype(jnp.bfloat16), (((1,), (1,)), ((), ())),
-            preferred_element_type=jnp.float32,
-        )
-        for g in range(groups):
-            hid_grad_ref[g, e] = slot_grad[g * pad:g * pad + capacity].astype(jnp.bfloat16)
+        gated.append((grad * gate[e:e + 1]).astype(jnp.bfloat16))
 
     returns = [
         pltpu.make_async_remote_copy(
@@ -121,7 +136,19 @@
     ]
     for copy in returns:
         copy.start()
-    for copy in sends:
+    gates_ref[...] = jnp.concatenate(
+        [gate, jnp.zeros((LANES - pad, tokens), jnp.float32)], axis=0
+    ).T
+    slot_grad = jnp.zeros((slot_rows, width), jnp.float32)
+    for e in range(exp_dev):
+        slot_grad = slot_grad + lax.dot_general(
+            picks[e], gated[e], (((1,), (1,)), ((), ())), preferred_element_type=jnp.float32
+        )
+    for g in range(groups):
+        for s in range(capacity):
+            at = (g * capacity + s) * pad
+            hid_grad_ref[g, s] = slot_grad[at:at + exp_dev].astype(jnp.bfloat16)
+    for copy in sends + swaps:
         copy.wait_send()
     for copy in returns:
         copy.wait_recv()
@@ -134,7 +161,12 @@
             total = total + jnp.where(d == me, mine, parts_in[d])
         for e in range(exp_dev):
             result = result + jnp.where(ids_t == p * exp_dev + e, total[e:e + 1], 0.0)
-    route_ref[...] = result
+    wanted = lax.broadcasted_iota(jnp.int32, (tok_dev, tokens), 0) + me * tok_dev
+    chosen = wanted == lax.broadcasted_iota(jnp.int32, (tok_dev, tokens), 1)
+    route_ref[...] = lax.dot_general(
+        jnp.where(chosen, 1.0, 0.0), result, (((1,), (1,)), ((), ())),
+        precision=HIGHEST, preferred_element_type=jnp.float32,
+    )
     for copy in returns:
         copy.wait_send()
 
@@ -159,37 +191,31 @@
     ctx_count, ep_count = lax.axis_size("ctx"), lax.axis_size("ep")
     count = ctx_count * ep_count
     tokens = count * tok_dev
-    pack = jnp.concatenate(
-        [
-            out_grad,
-            expert_ids.astype(jnp.bfloat16),
-            gate_values.astype(jnp.bfloat16),
-            jnp.zeros((tok_dev, LANES - 2 * top), jnp.bfloat16),
-        ],
-        axis=1,
-    )
     sizes = (ctx_count, ep_count, tok_dev, top, groups, exp_dev, capacity, width)
     vmem = pl.BlockSpec(memory_space=pltpu.VMEM)
     hid_grad, by_token, rows, gates, routes = pl.pallas_call(
         functools.partial(exchange_kernel, sizes),
         out_shape=(
-            jax.ShapeDtypeStruct(hidden.shape, jnp.bfloat16),
+            jax.ShapeDtypeStruct((groups, capacity, exp_dev, width), jnp.bfloat16),
             jax.ShapeDtypeStruct((exp_dev, width, tokens), jnp.bfloat16),
             jax.ShapeDtypeStruct((tokens, features), jnp.bfloat16),
             jax.ShapeDtypeStruct((tokens, LANES), jnp.float32),
-            jax.ShapeDtypeStruct((top, tokens), jnp.float32),
+            jax.ShapeDtypeStruct((tok_dev, top), jnp.float32),
         ),
-        in_specs=[vmem, vmem, pl.BlockSpec(memory_space=pl.ANY)],
+        in_specs=[vmem] * 4 + [pl.BlockSpec(memory_space=pl.ANY)],
         out_specs=(vmem,) * 5,
         scratch_shapes=[
+            pltpu.VMEM((tok_dev, features + LANES), jnp.bfloat16),
             pltpu.VMEM((count, tok_dev, features + LANES), jnp.bfloat16),
             pltpu.VMEM(w_down.shape, jnp.bfloat16),
             pltpu.VMEM((exp_dev, tokens), jnp.float32),
             pltpu.VMEM((count, exp_dev, tokens), jnp.float32),
             pltpu.SemaphoreType.DMA((exp_dev,)),
             pltpu.SemaphoreType.DMA,
-            pltpu.SemaphoreType.DMA((count - 1,)),
-            pltpu.SemaphoreType.DMA((count - 1,)),
+            pltpu.SemaphoreType.DMA((count // 2 - 1,)),
+            pltpu.SemaphoreType.DMA((count // 2 - 1,)),
+            pltpu.SemaphoreType.DMA((count // 2,)),
+            pltpu.SemaphoreType.DMA((count // 2,)),
             pltpu.SemaphoreType.DMA((count - 1,)),
             pltpu.SemaphoreType.DMA((count - 1,)),
         ],
@@ -197,7 +223,7 @@
             collective_id=0, has_side_effects=True, vmem_limit_bytes=56 << 20
         ),
         name="exchange",
-    )(pack, hidden, w_down)
+    )(out_grad, expert_ids, gate_values, jnp.transpose(hidden, (0, 2, 1, 3)), w_down)
     chunk = features
     for pieces in range(1, features // LANES + 1):
         if features % (pieces * LANES) == 0 and features // pieces <= 4 * LANES:
@@ -216,9 +242,7 @@
         compiler_params=pltpu.CompilerParams(vmem_limit_bytes=56 << 20),
         name="weight",
     )(by_token, rows, gates)
-    me = lax.axis_index("ctx") * ep_count + lax.axis_index("ep")
-    gate_grad = lax.dynamic_slice_in_dim(routes, me * tok_dev, tok_dev, 1).T
-    return hid_grad, weight_grad, gate_grad
+    return jnp.transpose(hid_grad, (0, 2, 1, 3)), weight_grad, routes
 
 
 def route_places(group_ids, experts_all, capacity):
@@ -293,7 +317,7 @@
     tokens = count * out_grad.shape[0]
     exp_dev = hidden.shape[1]
     held = 3 * 2 * tokens * out_grad.shape[1] + 2 * w_down.size + 32 * count * tokens
-    whole_tiles = out_grad.shape[1] % LANES == 0 and exp_dev <= 8 and hidden.shape[2] <= 8
+    whole_tiles = count % 2 == 0 and out_grad.shape[1] % LANES == 0 and exp_dev <= 8 and hidden.shape[2] <= 8
     body = fused_device if held <= VMEM_BUDGET and whole_tiles else plain_device
     return body(out_grad, expert_ids, gate_values, hidden, w_down)
 

time: 50 us -> 39.1 us (0.78)
  Pallas kernels: 41.7 us -> 37 us
  local copies, waits for them, and re-layouts: 5.89 us -> 1.21 us
  other arithmetic: 1.36 us -> 0 us
    pallas_call x1, Pallas kernels: 34.7 us -> 29.9 us  [fused_device(): pl.pallas_call(functools.partial(exchange_kernel, sizes), out_shape=(jax....]
    unnamed x3 -> x6, local copies, waits for them, and re-layouts: 3.74 us -> 1.21 us
    concatenate x1 -> x0, local copies, waits for them, and re-layouts: 1.4 us -> none  [fused_device(): jnp.concatenate([out_grad, expert_ids.astype(jnp.bfloat16), gate_values.a...]
    convert_element_type x2 -> x0, other arithmetic: 1.36 us -> none  [the longest x1 0.68 us: fused_device(): expert_ids.astype(jnp.bfloat16)]
    transpose x1 -> x0, local copies, waits for them, and re-layouts: 0.74 us -> none  [fused_device(): gate_grad = lax.dynamic_slice_in_dim(routes, me * tok_dev, tok_dev, 1).T]
where the time goes in v2:
time: 39.1 us; the launch traced here: 38.9 us
  Pallas kernels  37 us (95%)
  local copies, waits for them, and re-layouts  1.21 us (3%)
  between operations  0.66 us (2%)
    pallas_call x1, Pallas kernels, fused_device(): pl.pallas_call(functools.partial(exchange_kernel, sizes), out_shape=(jax....  29.9 us
    pallas_call x1, Pallas kernels, fused_device(): pl.pallas_call(functools.partial(weight_kernel, exp_dev, chunk), grid=(ex...  7.06 us
    unnamed x6, local copies, waits for them, and re-layouts  1.21 us

profile of v2, /device:TPU:0, one launch (start us, length us, event | category | flops | bytes accessed | tf_op | source)
XLA Modules:
  0.0 38.9 jit_solution(4734923007927111764)
XLA Ops:
  0.6 29.9 %exchange.1 = (bf16[4,7,4,384]{3,2,1,0:T(4,128)(2,1)}, bf16[4,384,64]{2,1,0:T(8,128)(2,1)}, bf16[64,3584]{1,0:T(8,128)(2,1)}, f32[64,128]{1,0:T(8,128)}, f32[2,8]{1,0:T(2,128)}) custom-call(bf16[2,3584]{1,0:T(2,128)(2,1)} %grad_ref.1, s32[2,8]{1,0:T(2,128)} %ids_ref.1, f32[2,8]{1,0:T(2,128)} %gate_ref.1, bf16[4,7,4,384]{3,2,1,0:T(4,128)(2,1)} %bitcast.2, ...), custom_call_target="tpu_custom_call" | custom-call | tf_op jit(solution)/shard_map/exchange/pallas_call | solution.py:196
  30.6 0.0 copy-start
  30.6 0.0 copy-start.1
  30.6 7.1 %weight.1 = bf16[4,384,3584]{2,1,0:T(8,128)(2,1)} custom-call(bf16[4,384,64]{2,1,0:T(8,128)(2,1)} %get-tuple-element.9.by_token_ref, bf16[64,3584]{1,0:T(8,128)(2,1)} %get-tuple-element.10.rows_ref, f32[64,128]{1,0:T(8,128)} %get-tuple-element.11.gates_ref), custom_call_target="tpu_custom_call" | custom-call | tf_op jit(solution)/shard_map/weight/pallas_call | solution.py:232
  37.7 0.0 copy-done
  37.7 0.6 %copy.10 = bf16[4,4,7,384]{3,1,2,0:T(4,128)(2,1)} copy(bf16[4,4,7,384]{3,1,2,0:T(4,128)(2,1)S(1)} %bitcast.3) | data formatting | bytes 172032
  38.3 0.0 copy-done.1
  38.3 0.6 %copy.11 = f32[2,8]{1,0:T(2,128)} copy(f32[2,8]{1,0:T(2,128)S(1)} %copy-done.1) | data formatting | bytes 128
Async XLA Ops:
  30.6 7.1 %copy-start = (bf16[4,7,4,384]{3,2,1,0:T(4,128)(2,1)S(1)}, bf16[4,7,4,384]{3,2,1,0:T(4,128)(2,1)}, u32[]{:S(2)}) copy-start(bf16[4,7,4,384]{3,2,1,0:T(4,128)(2,1)} %get-tuple-element.8) | copy-start | bytes 258052
  30.6 7.7 %copy-start.1 = (f32[2,8]{1,0:T(2,128)S(1)}, f32[2,8]{1,0:T(2,128)}, u32[]{:S(2)}) copy-start(f32[2,8]{1,0:T(2,128)} %get-tuple-element.18) | copy-start | bytes 196

commit v3 on v2

--- a/solution.py
+++ b/solution.py
@@ -30,7 +30,7 @@
         return (d // ep_count, lax.rem(d, ep_count))
 
     def rows_of(d):
-        return rows_in.at[d]
+        return rows_in.at[pl.ds(pl.multiple_of(d * tok_dev, tok_dev), tok_dev), :]
 
     peers = [place_of(lax.rem(me + step, count)) for step in range(1, count)]
     barrier = pltpu.get_barrier_semaphore()
@@ -95,7 +95,7 @@
     for copy in swaps:
         copy.wait_recv()
 
-    gathered = rows_in[...].reshape(tokens, features + LANES)
+    gathered = rows_in[...]
     rows_ref[...] = gathered[:, :features]
     meta_t = gathered[:, features:].astype(jnp.float32).T
     ids_t = meta_t[:top].astype(jnp.int32)
@@ -206,7 +206,7 @@
         out_specs=(vmem,) * 5,
         scratch_shapes=[
             pltpu.VMEM((tok_dev, features + LANES), jnp.bfloat16),
-            pltpu.VMEM((count, tok_dev, features + LANES), jnp.bfloat16),
+            pltpu.VMEM((tokens, features + LANES), jnp.bfloat16),
             pltpu.VMEM(w_down.shape, jnp.bfloat16),
             pltpu.VMEM((exp_dev, tokens), jnp.float32),
             pltpu.VMEM((count, exp_dev, tokens), jnp.float32),

time: 39.1 us -> 39.1 us (level)
  no operation moved by 1% of the time
where the time goes in v3:
time: 39.1 us; the launch traced here: 38.8 us
  Pallas kernels  37 us (95%)
  local copies, waits for them, and re-layouts  1.21 us (3%)
  between operations  0.66 us (2%)
    pallas_call x1, Pallas kernels, fused_device(): pl.pallas_call(functools.partial(exchange_kernel, sizes), out_shape=(jax....  29.9 us
    pallas_call x1, Pallas kernels, fused_device(): pl.pallas_call(functools.partial(weight_kernel, exp_dev, chunk), grid=(ex...  7.06 us
    unnamed x6, local copies, waits for them, and re-layouts  1.21 us

profile of v3, /device:TPU:0, one launch (start us, length us, event | category | flops | bytes accessed | tf_op | source)
XLA Modules:
  0.0 38.8 jit_solution(925591392687233243)
XLA Ops:
  0.6 29.9 %exchange.1 = (bf16[4,7,4,384]{3,2,1,0:T(4,128)(2,1)}, bf16[4,384,64]{2,1,0:T(8,128)(2,1)}, bf16[64,3584]{1,0:T(8,128)(2,1)}, f32[64,128]{1,0:T(8,128)}, f32[2,8]{1,0:T(2,128)}) custom-call(bf16[2,3584]{1,0:T(2,128)(2,1)} %grad_ref.1, s32[2,8]{1,0:T(2,128)} %ids_ref.1, f32[2,8]{1,0:T(2,128)} %gate_ref.1, bf16[4,7,4,384]{3,2,1,0:T(4,128)(2,1)} %bitcast.2, ...), custom_call_target="tpu_custom_call" | custom-call | tf_op jit(solution)/shard_map/exchange/pallas_call | solution.py:196
  30.5 0.0 copy-start
  30.6 0.0 copy-start.1
  30.6 7.1 %weight.1 = bf16[4,384,3584]{2,1,0:T(8,128)(2,1)} custom-call(bf16[4,384,64]{2,1,0:T(8,128)(2,1)} %get-tuple-element.9.by_token_ref, bf16[64,3584]{1,0:T(8,128)(2,1)} %get-tuple-element.10.rows_ref, f32[64,128]{1,0:T(8,128)} %get-tuple-element.11.gates_ref), custom_call_target="tpu_custom_call" | custom-call | tf_op jit(solution)/shard_map/weight/pallas_call | solution.py:232
  37.6 0.0 copy-done
  37.6 0.6 %copy.10 = bf16[4,4,7,384]{3,1,2,0:T(4,128)(2,1)} copy(bf16[4,4,7,384]{3,1,2,0:T(4,128)(2,1)S(1)} %bitcast.3) | data formatting | bytes 172032
  38.3 0.0 copy-done.1
  38.3 0.6 %copy.11 = f32[2,8]{1,0:T(2,128)} copy(f32[2,8]{1,0:T(2,128)S(1)} %copy-done.1) | data formatting | bytes 128
Async XLA Ops:
  30.5 7.1 %copy-start = (bf16[4,7,4,384]{3,2,1,0:T(4,128)(2,1)S(1)}, bf16[4,7,4,384]{3,2,1,0:T(4,128)(2,1)}, u32[]{:S(2)}) copy-start(bf16[4,7,4,384]{3,2,1,0:T(4,128)(2,1)} %get-tuple-element.8) | copy-start | bytes 258052
  30.6 7.7 %copy-start.1 = (f32[2,8]{1,0:T(2,128)S(1)}, f32[2,8]{1,0:T(2,128)}, u32[]{:S(2)}) copy-start(f32[2,8]{1,0:T(2,128)} %get-tuple-element.18) | copy-start | bytes 196
